TPU v7x, 32 devices: a whole 2x2x4 slice. The times are simulated.
32 devices in a mesh: ves: 16 (over z, y, x), sec: 2 (over core).
Axes of the slice: x: 2, y: 2, z: 4, core: 2. Of those that a mesh axis runs over, the one named last changes fastest.
Arguments:
- density: bfloat16 [8192, 3, 544], P(('ves', 'sec')), may hold values from -6 to 6
- analysis: bfloat16 [544, 289], replicated, may hold values from -0.25 to 0.25
- synthesis: bfloat16 [289, 544], replicated, may hold values from -0.375 to 0.375
- degree_gain: float32 [289], replicated, may hold values from 0.05 to 2
- near_kernel: bfloat16 [544, 544], replicated, may hold values from -0.25 to 0.25
- partners: int32 [8192, 4], P(('ves', 'sec')), may hold values from 0 to 8191, as said below
- pair_weight: float32 [8192, 4], P(('ves', 'sec')), may hold values from 0.2 to 1
- wall_list: int32 [512], P(('ves', 'sec')), may hold values from 0 to 8191, as said below
- coupling: bfloat16 [4096, 32], P(('ves', 'sec')), may hold values from -1 to 1
- wall_gain: float32 [4096], P(('ves', 'sec')), may hold values from 0.5 to 2
Outputs:
- velocity: float32 [8192, 3, 544], P(('ves', 'sec'))
Inputs may be any that keep to these rules, and one draw needn't show every extreme that they name: `partners`: vesicles form blocks of 256 consecutive ids, block b in region b // 2, slot b % 2. A partner of vesicle i lies in the block of i, or among the last 64 vesicles of the block of the region below with the same slot, or among the first 64 of the block of the region above with the same slot. No vesicle is its own partner. `wall_list`: entry block b (entries b * 16 to b * 16 + 15) holds 16 distinct ids of vesicle block b.
All inputs are finite; a program needn't handle non-finite values.
Results may differ from a plain program's by a relative error of at most 0.0043.
Values may be sent and summed in bfloat16 or wider, within the bound.
A program may use at most 64 MiB of HBM per device.

v0:
```python
import functools

import jax
import jax.numpy as jnp
from jax import lax
from jax.experimental import pallas as pl
from jax.experimental.pallas import tpu as pltpu
from jax.sharding import PartitionSpec as P

MESH = pl.DeviceIdType.MESH
F32 = jnp.float32
BF16 = jnp.bfloat16


def dot(a, b, ca=1, cb=0):
    return lax.dot_general(a, b, (((ca,), (cb,)), ((), ())), preferred_element_type=F32)


def step_kernel(
    n_ves,
    n_sec,
    dens_in,
    ana_in,
    syn_in,
    gain_ref,
    near_in,
    part_in,
    weight_in,
    list_in,
    coup_in,
    wgain_in,
    out_ref,
    dens_ref,
    ana_ref,
    syn_ref,
    near_ref,
    part_ref,
    weight_ref,
    list_ref,
    coup_ref,
    wgain_ref,
    syn_turned,
    both_ref,
    load_sem,
    coef_ref,
    mix_ref,
    total_ref,
    tail_ref,
    head_ref,
    recv_ref,
    pick_all,
    coup_all,
    gain_all,
    send_sem,
    recv_sem,
    wall_send,
    wall_recv,
):
    ves = lax.axis_index("ves")
    sec = lax.axis_index("sec")
    comps, _, count = dens_ref.shape
    num_coefs = ana_ref.shape[0]
    near_wall = list_ref.shape[0]
    edge = count // 4
    tile = 2 * edge
    cut = recv_ref.shape[2]
    top = num_coefs - cut
    has_left = ves > 0
    has_right = ves < n_ves - 1
    hops = range(1, n_sec)

    barrier = pltpu.get_barrier_semaphore()

    @pl.when(has_left)
    def _():
        pl.semaphore_signal(barrier, inc=1, device_id=(ves - 1, sec), device_id_type=MESH)

    @pl.when(has_right)
    def _():
        pl.semaphore_signal(barrier, inc=1, device_id=(ves + 1, sec), device_id_type=MESH)

    for hop in hops:
        peer = lax.rem(sec + hop, n_sec)
        pl.semaphore_signal(barrier, inc=1, device_id=(ves, peer), device_id_type=MESH)

    pairs = [(ana_in, ana_ref)]
    pairs += [(dens_in.at[c], dens_ref.at[c]) for c in range(comps)]
    pairs += [
        (list_in, list_ref),
        (part_in, part_ref),
        (weight_in, weight_ref),
        (coup_in, coup_ref),
        (wgain_in, wgain_ref),
        (syn_in, syn_ref),
        (near_in, near_ref),
    ]
    loads = [
        pltpu.make_async_copy(src, dst, load_sem.at[i]) for i, (src, dst) in enumerate(pairs)
    ]
    for load in loads[:-2]:
        load.start()
    load_ana, *load_dens = loads[: comps + 1]
    load_list, load_part, load_weight, load_coup, load_wgain, load_syn, load_near = loads[comps + 1 :]

    def halo_copy(src, side, c, to):
        return pltpu.make_async_remote_copy(
            src_ref=src.at[c],
            dst_ref=recv_ref.at[side, c],
            send_sem=send_sem.at[side, c],
            recv_sem=recv_sem.at[side, c],
            device_id=(to, sec),
            device_id_type=MESH,
        )

    def up_copy(c):
        return halo_copy(tail_ref, 0, c, ves + 1)

    def down_copy(c):
        return halo_copy(head_ref, 1, c, ves - 1)

    def wall_copy(hop, kind):
        src, dst = (
            (coup_in, coup_all.at[hop - 1]),
            (wgain_in, gain_all.at[hop - 1]),
            (pick_all.at[sec], pick_all.at[sec]),
        )[kind]
        return pltpu.make_async_remote_copy(
            src_ref=src,
            dst_ref=dst,
            send_sem=wall_send.at[kind, hop - 1],
            recv_sem=wall_recv.at[kind, hop - 1],
            device_id=(ves, lax.rem(sec + hop, n_sec)),
            device_id_type=MESH,
        )

    @pl.when(jnp.logical_not(has_left))
    def _():
        recv_ref[0] = jnp.zeros(recv_ref.shape[1:], BF16)

    @pl.when(jnp.logical_not(has_right))
    def _():
        recv_ref[1] = jnp.zeros(recv_ref.shape[1:], BF16)

    low = lax.broadcasted_iota(jnp.int32, (cut, tile), 1) < edge
    load_ana.wait()
    ana = ana_ref[...]

    for c in range(comps):
        load_dens[c].wait()
        full = dot(ana, dens_ref[c])
        coef_ref[c] = full.astype(BF16)
        head = full[:, :tile]
        tail = full[:, count - tile :]
        tail_ref[c] = jnp.where(low, pltpu.roll(tail, edge, 1)[:cut], tail[top:]).astype(BF16)
        head_ref[c] = jnp.where(low, head[:cut], pltpu.roll(head, edge, 1)[top:]).astype(BF16)
        if c == 0:
            sides = has_left.astype(jnp.int32) + has_right.astype(jnp.int32)
            pl.semaphore_wait(barrier, n_sec - 1 + sides)

        @pl.when(has_right)
        def _():
            up_copy(c).start()

        @pl.when(has_left)
        def _():
            down_copy(c).start()

        if c == 0:
            load_syn.start()
            load_near.start()

    for hop in hops:
        wall_copy(hop, 0).start()
        wall_copy(hop, 1).start()

    base = (ves * n_sec + sec) * count

    def placing(rows, first):
        row = lax.broadcasted_iota(jnp.int32, (rows, count), 0)
        ids = jnp.full((rows, count), -1, jnp.int32)
        for j in range(near_wall):
            ids = jnp.where(row == first + j, list_ref[j] - base, ids)
        hit = ids == lax.broadcasted_iota(jnp.int32, (rows, count), 1)
        return jnp.where(hit, 1.0, 0.0).astype(BF16)

    load_list.wait()
    choose = placing(near_wall, 0)
    for c in range(comps):
        pick_all[sec, c] = dot(choose, coef_ref[c], 1, 1).astype(BF16)
    for hop in hops:
        wall_copy(hop, 2).start()

    load_part.wait()
    load_weight.wait()
    shift = part_ref[...] - base
    weight = weight_ref[...]

    def mixing(rows, start):
        want = lax.broadcasted_iota(jnp.int32, (rows, count), 0) + start
        total = jnp.zeros((rows, count), F32)
        for k in range(shift.shape[0]):
            total = total + jnp.where(shift[k : k + 1, :] == want, weight[k : k + 1, :], 0.0)
        return total.astype(BF16)

    own_mix = mixing(count, 0)
    left_mix = mixing(edge, count - edge - n_sec * count)
    right_mix = mixing(edge, n_sec * count)
    none = jnp.zeros((edge, count), BF16)
    first_mix = jnp.concatenate([left_mix, none, right_mix, none], axis=0)
    second_mix = jnp.concatenate([none, left_mix, none, right_mix], axis=0)

    square = (num_coefs, num_coefs)
    diagonal = lax.broadcasted_iota(jnp.int32, square, 0) == lax.broadcasted_iota(
        jnp.int32, square, 1
    )
    gain = jnp.sum(jnp.where(diagonal, gain_ref[...].reshape(1, num_coefs), 0.0), axis=1, keepdims=True)

    for c in range(comps):
        mix_ref[c] = dot(coef_ref[c], own_mix)

    load_syn.wait()
    syn_turned[...] = syn_ref[...].T
    syn = syn_turned[...]
    load_near.wait()
    both_ref[...] = dot(near_ref[...].T, syn).astype(BF16)

    for hop in hops:
        for kind in range(3):
            wall_copy(hop, kind).wait()
    load_coup.wait()
    load_wgain.wait()
    coup = jnp.concatenate([coup_ref[...]] + [coup_all[hop - 1] for hop in hops], axis=1)
    wgain = jnp.concatenate([wgain_ref[...]] + [gain_all[hop - 1] for hop in hops], axis=1)
    place = placing(near_wall * n_sec, sec * near_wall)
    for c in range(comps):
        picked = jnp.concatenate([pick_all[s, c] for s in range(n_sec)], axis=0)
        dens = (dot(picked, coup, 0, 0) * wgain).astype(BF16)
        back = dot(coup, dens, 1, 1).astype(BF16)
        wall = dot(back, place, 0, 0)
        scaled = coef_ref[c].astype(F32) * gain
        out_ref[c] = dot(syn, (scaled + wall).astype(BF16))

    def receive(c):
        @pl.when(has_left)
        def _():
            up_copy(c).wait_recv()

        @pl.when(has_right)
        def _():
            down_copy(c).wait_recv()

    for c in range(comps):
        receive(c)
        halo = jnp.concatenate([recv_ref[0, c], recv_ref[1, c]], axis=1)
        first = dot(halo[:top], first_mix)
        second = dot(halo, second_mix)
        total_ref[:top] = (mix_ref[c, :top] + first).astype(BF16)
        total_ref[top:] = (mix_ref[c, top:] + second).astype(BF16)
        total = total_ref[...]
        out_ref[c] = out_ref[c] + dot(both_ref[...], total)

    for c in range(comps):

        @pl.when(has_right)
        def _():
            up_copy(c).wait_send()

        @pl.when(has_left)
        def _():
            down_copy(c).wait_send()


def shards(
    n_ves,
    n_sec,
    density,
    analysis,
    synthesis,
    degree_gain,
    near_kernel,
    partners,
    pair_weight,
    wall_list,
    coupling,
    wall_gain,
):
    count, comps, num_points = density.shape
    num_coefs = analysis.shape[1]
    near_wall = wall_list.shape[0]
    panels, region_wall = coupling.shape
    tile = count // 2
    top = num_coefs // 2 // 16 * 16
    cut = num_coefs - top
    others = max(n_sec - 1, 1)
    vmem = pl.BlockSpec(memory_space=pltpu.VMEM)
    specs = [pl.BlockSpec(memory_space=pltpu.HBM)] * 10
    specs[3] = vmem
    out = pl.pallas_call(
        functools.partial(step_kernel, n_ves, n_sec),
        name="vesicle_step",
        out_shape=jax.ShapeDtypeStruct((comps, num_points, count), F32),
        in_specs=specs,
        out_specs=vmem,
        scratch_shapes=[
            pltpu.VMEM((comps, num_points, count), BF16),
            pltpu.VMEM((num_coefs, num_points), BF16),
            pltpu.VMEM((num_coefs, num_points), BF16),
            pltpu.VMEM((num_points, num_points), BF16),
            pltpu.VMEM(partners.shape[::-1], jnp.int32),
            pltpu.VMEM(partners.shape[::-1], F32),
            pltpu.SMEM((near_wall,), jnp.int32),
            pltpu.VMEM((region_wall, panels), BF16),
            pltpu.VMEM((1, panels), F32),
            pltpu.VMEM((num_points, num_coefs), BF16),
            pltpu.VMEM((num_points, num_coefs), BF16),
            pltpu.SemaphoreType.DMA((comps + 8,)),
            pltpu.VMEM((comps, num_coefs, count), BF16),
            pltpu.VMEM((comps, num_coefs, count), F32),
            pltpu.VMEM((num_coefs, count), BF16),
            pltpu.VMEM((comps, cut, tile), BF16),
            pltpu.VMEM((comps, cut, tile), BF16),
            pltpu.VMEM((2, comps, cut, tile), BF16),
            pltpu.VMEM((n_sec, comps, near_wall, num_coefs), BF16),
            pltpu.VMEM((others, region_wall, panels), BF16),
            pltpu.VMEM((others, 1, panels), F32),
            pltpu.SemaphoreType.DMA((2, comps)),
            pltpu.SemaphoreType.DMA((2, comps)),
            pltpu.SemaphoreType.DMA((3, others)),
            pltpu.SemaphoreType.DMA((3, others)),
        ],
        compiler_params=pltpu.CompilerParams(
            collective_id=0, has_side_effects=True, vmem_limit_bytes=32 * 1024 * 1024
        ),
    )(
        *(
            pltpu.with_memory_space_constraint(array, pltpu.HBM)
            for array in (
                density.transpose(1, 2, 0),
                analysis.T,
                synthesis,
                degree_gain,
                near_kernel,
                partners.T,
                pair_weight.T,
                wall_list,
                coupling.T,
                wall_gain.reshape(1, panels),
            )
        )
    )
    return out.transpose(2, 0, 1)


def solution(mesh):
    n_ves, n_sec = mesh.shape["ves"], mesh.shape["sec"]
    return jax.shard_map(
        functools.partial(shards, n_ves, n_sec),
        mesh=mesh,
        in_specs=(
            P(("ves", "sec"), None, None),
            P(),
            P(),
            P(),
            P(),
            P(("ves", "sec"), None),
            P(("ves", "sec"), None),
            P(("ves", "sec")),
            P(("ves", "sec"), None),
            P(("ves", "sec")),
        ),
        out_specs=P(("ves", "sec"), None, None),
        check_vma=False,
    )
```

profile of v0, /device:TPU:0, one launch (start us, length us, event | category | flops | bytes accessed | tf_op | source)
XLA Modules:
  0.0 12.9 jit_solution(7051003170579590429)
XLA Ops:
  0.0 11.7 %vesicle_step.1 = f32[3,544,256]{2,1,0:T(8,128)S(1)} custom-call(bf16[3,544,256]{2,1,0:T(8,128)(2,1)} %bitcast.8, bf16[289,544]{1,0:T(8,128)(2,1)} %bitcast.9, bf16[289,544]{1,0:T(8,128)(2,1)} %syn_in.1, f32[289]{0:T(512)} %gain_ref.1, bf16[544,544]{1,0:T(8,128)(2,1)} %near_in.1, s32[4,256]{1,0:T(4,128)} %bitcast.11, f32[4,256]{1,0:T(4,128)} %bitcast.12, ...), custom_call_target="tpu_custom_call" | custom-call | tf_op jit(solution)/shard_map/vesicle_step/pallas_call | solution.py:298
  11.7 1.2 %copy.12 = f32[256,3,544]{0,2,1:T(8,128)} copy(f32[256,3,544]{0,2,1:T(8,128)S(1)} %bitcast.7) | data formatting | bytes 3342336
where the time goes:
time: 13.1 us; the launch traced here: 12.9 us
  Pallas kernels  11.7 us (89%)
  local copies, waits for them, and re-layouts  1.18 us (9%)
    pallas_call x1, Pallas kernels, shards(): pl.pallas_call(functools.partial(step_kernel, n_ves, n_sec), name='vesicl...  11.7 us
    unnamed x1, local copies, waits for them, and re-layouts  1.18 us

commit v1 on v0

--- a/solution.py
+++ b/solution.py
@@ -22,7 +22,7 @@
     dens_in,
     ana_in,
     syn_in,
-    gain_ref,
+    gain_in,
     near_in,
     part_in,
     weight_in,
@@ -39,6 +39,7 @@
     list_ref,
     coup_ref,
     wgain_ref,
+    gain_ref,
     syn_turned,
     both_ref,
     load_sem,
@@ -91,6 +92,7 @@
         (weight_in, weight_ref),
         (coup_in, coup_ref),
         (wgain_in, wgain_ref),
+        (gain_in, gain_ref),
         (syn_in, syn_ref),
         (near_in, near_ref),
     ]
@@ -100,7 +102,7 @@
     for load in loads[:-2]:
         load.start()
     load_ana, *load_dens = loads[: comps + 1]
-    load_list, load_part, load_weight, load_coup, load_wgain, load_syn, load_near = loads[comps + 1 :]
+    load_list, load_part, load_weight, load_coup, load_wgain, load_gain, load_syn, load_near = loads[comps + 1 :]
 
     def halo_copy(src, side, c, to):
         return pltpu.make_async_remote_copy(
@@ -145,6 +147,23 @@
     load_ana.wait()
     ana = ana_ref[...]
 
+    far_up = lax.rem(ves, 2) == 1
+    up_first = ves != 1
+
+    def send_up(c, cond):
+        @pl.when(jnp.logical_and(has_right, cond))
+        def _():
+            up_copy(c).start()
+
+    def send_down(c, cond):
+        @pl.when(jnp.logical_and(has_left, cond))
+        def _():
+            down_copy(c).start()
+
+    def greet():
+        sides = has_left.astype(jnp.int32) + has_right.astype(jnp.int32)
+        pl.semaphore_wait(barrier, n_sec - 1 + sides)
+
     for c in range(comps):
         load_dens[c].wait()
         full = dot(ana, dens_ref[c])
@@ -154,20 +173,24 @@
         tail_ref[c] = jnp.where(low, pltpu.roll(tail, edge, 1)[:cut], tail[top:]).astype(BF16)
         head_ref[c] = jnp.where(low, head[:cut], pltpu.roll(head, edge, 1)[top:]).astype(BF16)
         if c == 0:
-            sides = has_left.astype(jnp.int32) + has_right.astype(jnp.int32)
-            pl.semaphore_wait(barrier, n_sec - 1 + sides)
-
-        @pl.when(has_right)
-        def _():
-            up_copy(c).start()
-
-        @pl.when(has_left)
-        def _():
-            down_copy(c).start()
-
-        if c == 0:
+            @pl.when(has_left)
+            def _():
+                greet()
             load_syn.start()
             load_near.start()
+        send_up(c, jnp.logical_and(up_first, has_left))
+        send_down(c, True)
+
+    @pl.when(jnp.logical_not(has_left))
+    def _():
+        greet()
+
+    for c in range(comps):
+        send_up(c, jnp.logical_not(up_first))
+    for c in range(comps):
+        @pl.when(jnp.logical_not(has_left))
+        def _():
+            up_copy(c).start()
 
     for hop in hops:
         wall_copy(hop, 0).start()
@@ -209,6 +232,7 @@
     first_mix = jnp.concatenate([left_mix, none, right_mix, none], axis=0)
     second_mix = jnp.concatenate([none, left_mix, none, right_mix], axis=0)
 
+    load_gain.wait()
     square = (num_coefs, num_coefs)
     diagonal = lax.broadcasted_iota(jnp.int32, square, 0) == lax.broadcasted_iota(
         jnp.int32, square, 1
@@ -294,7 +318,6 @@
     others = max(n_sec - 1, 1)
     vmem = pl.BlockSpec(memory_space=pltpu.VMEM)
     specs = [pl.BlockSpec(memory_space=pltpu.HBM)] * 10
-    specs[3] = vmem
     out = pl.pallas_call(
         functools.partial(step_kernel, n_ves, n_sec),
         name="vesicle_step",
@@ -311,9 +334,10 @@
             pltpu.SMEM((near_wall,), jnp.int32),
             pltpu.VMEM((region_wall, panels), BF16),
             pltpu.VMEM((1, panels), F32),
+            pltpu.VMEM((num_coefs,), F32),
             pltpu.VMEM((num_points, num_coefs), BF16),
             pltpu.VMEM((num_points, num_coefs), BF16),
-            pltpu.SemaphoreType.DMA((comps + 8,)),
+            pltpu.SemaphoreType.DMA((comps + 9,)),
             pltpu.VMEM((comps, num_coefs, count), BF16),
             pltpu.VMEM((comps, num_coefs, count), F32),
             pltpu.VMEM((num_coefs, count), BF16),

time: 13.1 us -> 11.3 us (0.86)
  the two profiles are of different devices: /device:TPU:0 before, /device:TPU:4 now
where the time goes in v1:
time: 11.3 us; the launch traced here: 11.1 us
  Pallas kernels  9.93 us (88%)
  local copies, waits for them, and re-layouts  1.18 us (10%)
    pallas_call x1, Pallas kernels, shards(): pl.pallas_call(functools.partial(step_kernel, n_ves, n_sec), name='vesicl...  9.93 us
    unnamed x1, local copies, waits for them, and re-layouts  1.18 us

profile of v1, /device:TPU:4, one launch (start us, length us, event | category | flops | bytes accessed | tf_op | source)
XLA Modules:
  0.0 11.1 jit_solution(2674570944716401430)
XLA Ops:
  0.0 9.9 %vesicle_step.1 = f32[3,544,256]{2,1,0:T(8,128)S(1)} custom-call(bf16[3,544,256]{2,1,0:T(8,128)(2,1)} %bitcast.8, bf16[289,544]{1,0:T(8,128)(2,1)} %bitcast.9, bf16[289,544]{1,0:T(8,128)(2,1)} %syn_in.1, f32[289]{0:T(512)} %gain_in.1, bf16[544,544]{1,0:T(8,128)(2,1)} %near_in.1, s32[4,256]{1,0:T(4,128)} %bitcast.11, f32[4,256]{1,0:T(4,128)} %bitcast.12, ...), custom_call_target="tpu_custom_call" | custom-call | tf_op jit(solution)/shard_map/vesicle_step/pallas_call | solution.py:321
  9.9 1.2 %copy.12 = f32[256,3,544]{0,2,1:T(8,128)} copy(f32[256,3,544]{0,2,1:T(8,128)S(1)} %bitcast.7) | data formatting | bytes 3342336

commit v2 on v0

v2 whole, which is shorter than its diff:
```python
import functools

import jax
import jax.numpy as jnp
from jax import lax
from jax.experimental import pallas as pl
from jax.experimental.pallas import tpu as pltpu
from jax.sharding import PartitionSpec as P

MESH = pl.DeviceIdType.MESH
F32 = jnp.float32
BF16 = jnp.bfloat16


def dot(a, b, ca=1, cb=0):
    return lax.dot_general(a, b, (((ca,), (cb,)), ((), ())), preferred_element_type=F32)


def dot_rows(a, b, cut):
    return jnp.concatenate([dot(a[:cut], b), dot(a[cut:], b)], axis=0)


def halo_mix(recv_ref, spread_ref, c, top):
    halo = jnp.concatenate([recv_ref[0, c], recv_ref[1, c]], axis=1)
    return dot(halo[:top], spread_ref[0]), dot(halo, spread_ref[1])


def step_kernel(
    n_ves,
    n_sec,
    dens_in,
    ana_in,
    syn_in,
    gain_in,
    near_in,
    part_in,
    weight_in,
    list_in,
    coup_in,
    wgain_in,
    out_ref,
    both_ref,
    mix_ref,
    total_ref,
    spread_ref,
    recv_ref,
    dens_ref,
    ana_ref,
    syn_ref,
    near_ref,
    part_ref,
    weight_ref,
    list_ref,
    coup_ref,
    wgain_ref,
    gain_ref,
    syn_turned,
    coef_ref,
    tail_ref,
    head_ref,
    pick_all,
    coup_all,
    gain_all,
    send_sem,
    recv_sem,
    wall_recv,
):
    ves = lax.axis_index("ves")
    sec = lax.axis_index("sec")
    comps, _, count = dens_ref.shape
    num_coefs = ana_ref.shape[0]
    near_wall = list_ref.shape[0]
    edge = count // 4
    tile = 2 * edge
    cut = recv_ref.shape[2]
    top = num_coefs - cut
    half = out_ref.shape[1] // 2
    has_left = ves > 0
    has_right = ves < n_ves - 1
    hops = range(1, n_sec)

    barrier = pltpu.get_barrier_semaphore()

    @pl.when(has_left)
    def _():
        pl.semaphore_signal(barrier, inc=1, device_id=(ves - 1, sec), device_id_type=MESH)

    @pl.when(has_right)
    def _():
        pl.semaphore_signal(barrier, inc=1, device_id=(ves + 1, sec), device_id_type=MESH)

    for hop in hops:
        peer = lax.rem(sec + hop, n_sec)
        pl.semaphore_signal(barrier, inc=1, device_id=(ves, peer), device_id_type=MESH)

    def halo_copy(src, side, part, to):
        return pltpu.make_async_remote_copy(
            src_ref=src.at[part],
            dst_ref=recv_ref.at[side, part],
            send_sem=send_sem.at[side],
            recv_sem=recv_sem.at[side, part],
            device_id=(to, sec),
            device_id_type=MESH,
        )

    def up_copy(c):
        return halo_copy(tail_ref, 0, c, ves + 1)

    def down_copy(c):
        return halo_copy(head_ref, 1, c, ves - 1)

    turn = lax.rem(ves, 4)
    up_first = (turn == 0)
    greet_stage = jnp.where(ves == 0, jnp.where(sec == 0, 4, 2), jnp.where(turn == 0, 2, jnp.where(turn == 1, 0, jnp.where(turn == 2, 0, 0))))
    second_stage = jnp.where(ves == 0, jnp.where(sec == 0, 4, 3), jnp.where(turn == 0, 5, jnp.where(turn == 1, jnp.where(sec == 0, 2, 4), jnp.where(turn == 2, 3, 3))))

    def send(c, lead, when):
        up = up_first if lead else jnp.logical_not(up_first)

        @pl.when(when & has_right & up)
        def _():
            up_copy(c).start()

        @pl.when(when & has_left & jnp.logical_not(up))
        def _():
            down_copy(c).start()

    def at_stage(stage):
        @pl.when(greet_stage == stage)
        def _():
            sides = has_left.astype(jnp.int32) + has_right.astype(jnp.int32)
            pl.semaphore_wait(barrier, n_sec - 1 + sides)

        for c in range(comps):
            if c == stage:
                send(c, True, greet_stage <= stage)
            elif c < stage:
                send(c, True, greet_stage == stage)
        if stage >= comps - 1:
            for c in range(comps):
                send(c, False, second_stage == stage)

    def work(load_sem, wall_send):
        pairs = [(ana_in, ana_ref)]
        pairs += [(dens_in.at[c], dens_ref.at[c]) for c in range(comps)]
        pairs += [
            (list_in, list_ref),
            (part_in, part_ref),
            (weight_in, weight_ref),
            (coup_in, coup_ref),
            (wgain_in, wgain_ref),
            (gain_in, gain_ref),
            (syn_in, syn_ref),
            (near_in, near_ref),
        ]
        loads = [
            pltpu.make_async_copy(src, dst, load_sem.at[i]) for i, (src, dst) in enumerate(pairs)
        ]
        for load in loads[:-2]:
            load.start()
        load_ana, *load_dens = loads[: comps + 1]
        load_list, load_part, load_weight, load_coup, load_wgain, load_gain, load_syn, load_near = (
            loads[comps + 1 :]
        )

        def wall_copy(hop, kind):
            src, dst = (
                (coup_in, coup_all.at[hop - 1]),
                (wgain_in, gain_all.at[hop - 1]),
                (pick_all.at[sec], pick_all.at[sec]),
            )[kind]
            return pltpu.make_async_remote_copy(
                src_ref=src,
                dst_ref=dst,
                send_sem=wall_send.at[kind, hop - 1],
                recv_sem=wall_recv.at[kind, hop - 1],
                device_id=(ves, lax.rem(sec + hop, n_sec)),
                device_id_type=MESH,
            )

        def send_walls(when):
            @pl.when(when)
            def _():
                for hop in hops:
                    for kind in (2, 0, 1):
                        wall_copy(hop, kind).start()

        @pl.when(jnp.logical_not(has_left))
        def _():
            recv_ref[0] = jnp.zeros(recv_ref.shape[1:], BF16)

        @pl.when(jnp.logical_not(has_right))
        def _():
            recv_ref[1] = jnp.zeros(recv_ref.shape[1:], BF16)

        low = lax.broadcasted_iota(jnp.int32, (cut, tile), 1) < edge
        load_ana.wait()
        ana = ana_ref[...]

        for c in range(comps):
            load_dens[c].wait()
            full = dot_rows(ana, dens_ref[c], top)
            coef_ref[c] = full.astype(BF16)
            head = full[:, :tile]
            tail = full[:, count - tile :]
            tail_ref[c] = jnp.where(low, pltpu.roll(tail, edge, 1)[:cut], tail[top:]).astype(BF16)
            head_ref[c] = jnp.where(low, head[:cut], pltpu.roll(head, edge, 1)[top:]).astype(BF16)
            if c == 0:
                load_syn.start()
                load_near.start()
            at_stage(c)

        base = (ves * n_sec + sec) * count

        def placing(rows, first):
            row = lax.broadcasted_iota(jnp.int32, (rows, count), 0)
            ids = jnp.full((rows, count), -1, jnp.int32)
            for j in range(near_wall):
                ids = jnp.where(row == first + j, list_ref[j] - base, ids)
            hit = ids == lax.broadcasted_iota(jnp.int32, (rows, count), 1)
            return jnp.where(hit, 1.0, 0.0).astype(BF16)

        load_list.wait()
        choose = placing(near_wall, 0)
        for c in range(comps):
            pick_all[sec, c] = dot(choose, coef_ref[c], 1, 1).astype(BF16)
        at_stage(comps)
        send_walls(greet_stage <= comps)

        load_part.wait()
        load_weight.wait()
        shift = part_ref[...] - base
        weight = weight_ref[...]

        def mixing(rows, start):
            want = lax.broadcasted_iota(jnp.int32, (rows, count), 0) + start
            total = jnp.zeros((rows, count), F32)
            for k in range(shift.shape[0]):
                total = total + jnp.where(shift[k : k + 1, :] == want, weight[k : k + 1, :], 0.0)
            return total.astype(BF16)

        own_mix = mixing(count, 0)
        left_mix = mixing(edge, count - edge - n_sec * count)
        right_mix = mixing(edge, n_sec * count)
        none = jnp.zeros((edge, count), BF16)
        spread_ref[0] = jnp.concatenate([left_mix, none, right_mix, none], axis=0)
        spread_ref[1] = jnp.concatenate([none, left_mix, none, right_mix], axis=0)

        load_gain.wait()
        square = (num_coefs, num_coefs)
        diagonal = lax.broadcasted_iota(jnp.int32, square, 0) == lax.broadcasted_iota(
            jnp.int32, square, 1
        )
        gain = jnp.sum(
            jnp.where(diagonal, gain_ref[...].reshape(1, num_coefs), 0.0), axis=1, keepdims=True
        )

        for c in range(comps):
            mix_ref[c] = dot(coef_ref[c], own_mix)
        at_stage(comps + 1)
        send_walls(greet_stage > comps)

        load_syn.wait()
        syn_turned[...] = syn_ref[...].T
        syn = syn_turned[...]
        load_near.wait()
        both_ref[...] = dot(near_ref[...].T, syn).astype(BF16)
        at_stage(comps + 2)

        for hop in hops:
            for kind in range(3):
                wall_copy(hop, kind).wait()
        load_coup.wait()
        load_wgain.wait()
        coup = jnp.concatenate([coup_ref[...]] + [coup_all[hop - 1] for hop in hops], axis=1)
        wgain = jnp.concatenate([wgain_ref[...]] + [gain_all[hop - 1] for hop in hops], axis=1)
        place = placing(near_wall * n_sec, sec * near_wall)
        for c in range(comps):
            picked = jnp.concatenate([pick_all[s, c] for s in range(n_sec)], axis=0)
            dens = (dot(picked, coup, 0, 0) * wgain).astype(BF16)
            back = dot(coup, dens, 1, 1).astype(BF16)
            wall = dot(back, place, 0, 0)
            scaled = coef_ref[c].astype(F32) * gain
            out_ref[c] = dot_rows(syn, (scaled + wall).astype(BF16), half)

    pl.run_scoped(
        work,
        pltpu.SemaphoreType.DMA((comps + 9,)),
        pltpu.SemaphoreType.DMA((3, max(n_sec - 1, 1))),
    )

    for c in range(comps):

        @pl.when(has_left)
        def _():
            up_copy(c).wait_recv()

        @pl.when(has_right)
        def _():
            down_copy(c).wait_recv()

        if c < comps - 1:
            first, second = halo_mix(recv_ref, spread_ref, c, top)
            total_ref[:top] = (mix_ref[c, :top] + first).astype(BF16)
            total_ref[top:] = (mix_ref[c, top:] + second).astype(BF16)
        if c < comps - 2:
            out_ref[c] = out_ref[c] + dot_rows(both_ref[...], total_ref[...], half)

    @pl.when(has_right)
    def _():
        pltpu.make_async_remote_copy(
            src_ref=tail_ref, dst_ref=recv_ref.at[0], send_sem=send_sem.at[0], recv_sem=recv_sem.at[0, 0],
            device_id=(ves + 1, sec), device_id_type=MESH,
        ).wait_send()

    @pl.when(has_left)
    def _():
        pltpu.make_async_remote_copy(
            src_ref=head_ref, dst_ref=recv_ref.at[1], send_sem=send_sem.at[1], recv_sem=recv_sem.at[1, 0],
            device_id=(ves - 1, sec), device_id_type=MESH,
        ).wait_send()


def finish_kernel(
    part_ref,
    both_ref,
    mix_ref,
    total_ref,
    spread_ref,
    recv_ref,
    out_ref,
    result_ref,
    last_ref,
    done_sem,
    piece_sem,
):
    comps, num_points, _ = part_ref.shape
    last = comps - 1
    top = mix_ref.shape[1] - recv_ref.shape[2]
    half = num_points // 2
    stores = [
        pltpu.make_async_copy(part_ref.at[c], out_ref.at[c], done_sem.at[c])
        for c in range(comps - 2)
    ]
    for store in stores:
        store.start()
    first, second = halo_mix(recv_ref, spread_ref, last, top)
    last_ref[:top] = (mix_ref[last, :top] + first).astype(BF16)
    last_ref[top:] = (mix_ref[last, top:] + second).astype(BF16)
    for k, source in enumerate((total_ref, last_ref)):
        c = comps - 2 + k
        total = source[...]
        for i in range(2):
            rows = pl.ds(i * half, half)
            result_ref[k, rows] = part_ref[c, rows] + dot(both_ref[rows], total)
            store = pltpu.make_async_copy(
                result_ref.at[k, rows], out_ref.at[c, rows], piece_sem.at[k, i]
            )
            store.start()
            stores.append(store)
    for store in stores:
        store.wait()


def shards(
    n_ves,
    n_sec,
    density,
    analysis,
    synthesis,
    degree_gain,
    near_kernel,
    partners,
    pair_weight,
    wall_list,
    coupling,
    wall_gain,
):
    count, comps, num_points = density.shape
    num_coefs = analysis.shape[1]
    near_wall = wall_list.shape[0]
    panels, region_wall = coupling.shape
    tile = count // 2
    top = num_coefs // 2 // 16 * 16
    cut = num_coefs - top
    others = max(n_sec - 1, 1)
    vmem = pl.BlockSpec(memory_space=pltpu.VMEM)
    middle = pl.pallas_call(
        functools.partial(step_kernel, n_ves, n_sec),
        name="vesicle_step",
        out_shape=(
            jax.ShapeDtypeStruct((comps, num_points, count), F32),
            jax.ShapeDtypeStruct((num_points, num_coefs), BF16),
            jax.ShapeDtypeStruct((comps, num_coefs, count), F32),
            jax.ShapeDtypeStruct((num_coefs, count), BF16),
            jax.ShapeDtypeStruct((2, 2 * tile, count), BF16),
            jax.ShapeDtypeStruct((2, comps, cut, tile), BF16),
        ),
        in_specs=[pl.BlockSpec(memory_space=pltpu.HBM)] * 10,
        out_specs=[vmem] * 6,
        scratch_shapes=[
            pltpu.VMEM((comps, num_points, count), BF16),
            pltpu.VMEM((num_coefs, num_points), BF16),
            pltpu.VMEM((num_coefs, num_points), BF16),
            pltpu.VMEM((num_points, num_points), BF16),
            pltpu.VMEM(partners.shape[::-1], jnp.int32),
            pltpu.VMEM(partners.shape[::-1], F32),
            pltpu.SMEM((near_wall,), jnp.int32),
            pltpu.VMEM((region_wall, panels), BF16),
            pltpu.VMEM((1, panels), F32),
            pltpu.VMEM((num_coefs,), F32),
            pltpu.VMEM((num_points, num_coefs), BF16),
            pltpu.VMEM((comps, num_coefs, count), BF16),
            pltpu.VMEM((comps, cut, tile), BF16),
            pltpu.VMEM((comps, cut, tile), BF16),
            pltpu.VMEM((n_sec, comps, near_wall, num_coefs), BF16),
            pltpu.VMEM((others, region_wall, panels), BF16),
            pltpu.VMEM((others, 1, panels), F32),
            pltpu.SemaphoreType.DMA((2,)),
            pltpu.SemaphoreType.DMA((2, comps)),
            pltpu.SemaphoreType.DMA((3, others)),
        ],
        compiler_params=pltpu.CompilerParams(
            collective_id=0, has_side_effects=True, vmem_limit_bytes=32 * 1024 * 1024
        ),
    )(
        *(
            pltpu.with_memory_space_constraint(array, pltpu.HBM)
            for array in (
                density.transpose(1, 2, 0),
                analysis.T,
                synthesis,
                degree_gain,
                near_kernel,
                partners.T,
                pair_weight.T,
                wall_list,
                coupling.T,
                wall_gain.reshape(1, panels),
            )
        )
    )
    out = pl.pallas_call(
        finish_kernel,
        name="vesicle_finish",
        out_shape=jax.ShapeDtypeStruct((comps, num_points, count), F32),
        in_specs=[vmem] * 6,
        out_specs=pl.BlockSpec(memory_space=pltpu.HBM),
        scratch_shapes=[
            pltpu.VMEM((2, num_points, count), F32),
            pltpu.VMEM((num_coefs, count), BF16),
            pltpu.SemaphoreType.DMA((comps - 2,)),
            pltpu.SemaphoreType.DMA((2, 2)),
        ],
        compiler_params=pltpu.CompilerParams(vmem_limit_bytes=16 * 1024 * 1024),
    )(*middle)
    return out.transpose(2, 0, 1)


def solution(mesh):
    n_ves, n_sec = mesh.shape["ves"], mesh.shape["sec"]
    return jax.shard_map(
        functools.partial(shards, n_ves, n_sec),
        mesh=mesh,
        in_specs=(
            P(("ves", "sec"), None, None),
            P(),
            P(),
            P(),
            P(),
            P(("ves", "sec"), None),
            P(("ves", "sec"), None),
            P(("ves", "sec")),
            P(("ves", "sec"), None),
            P(("ves", "sec")),
        ),
        out_specs=P(("ves", "sec"), None, None),
        check_vma=False,
    )
```

time: 13.1 us -> 10.3 us (0.79)
  the two profiles are of different devices: /device:TPU:0 before, /device:TPU:4 now
where the time goes in v2:
time: 10.3 us; the launch traced here: 10.1 us
  Pallas kernels  10.1 us (98%)
    pallas_call x1, Pallas kernels, shards(): pl.pallas_call(functools.partial(step_kernel, n_ves, n_sec), name='vesicl...  8.67 us
    pallas_call x1, Pallas kernels, shards(): pl.pallas_call(finish_kernel, name='vesicle_finish', out_shape=jax.ShapeD...  1.39 us

profile of v2, /device:TPU:4, one launch (start us, length us, event | category | flops | bytes accessed | tf_op | source)
XLA Modules:
  0.0 10.1 jit_solution(9942517118267002479)
XLA Ops:
  0.0 8.7 %vesicle_step.1 = (f32[3,544,256]{2,1,0:T(8,128)S(1)}, bf16[544,289]{1,0:T(8,128)(2,1)S(1)}, f32[3,289,256]{2,1,0:T(8,128)S(1)}, bf16[289,256]{1,0:T(8,128)(2,1)...) custom-call(bf16[3,544,256]{2,1,0:T(8,128)(2,1)} %bitcast.7, bf16[289,544]{1,0:T(8,128)(2,1)} %bitcast.8, ...), custom_call_target="tpu_custom_call" | custom-call | tf_op jit(solution)/shard_map/vesicle_step/pallas_call | solution.py:388
  8.7 1.4 %vesicle_finish.1 = f32[3,544,256]{2,1,0:T(8,128)} custom-call(f32[3,544,256]{2,1,0:T(8,128)S(1)} %get-tuple-element.11.part_ref, bf16[544,289]{1,0:T(8,128)(2,1)S(1)} %get-tuple-element.12.both_ref, f32[3,289,256]{2,1,0:T(8,128)S(1)} %get-tuple-element.13.mix_ref, bf16[289,256]{1,0:T(8,128)(2,1)S(1)} %get-tuple-element.14.total_ref, ...), custom_call_target="tpu_custom_call" | custom-call | tf_op jit(solution)/shard_map/vesicle_finish/pallas_call | solution.py:443

commit v3 on v2

--- a/solution.py
+++ b/solution.py
@@ -11,18 +11,19 @@
 F32 = jnp.float32
 BF16 = jnp.bfloat16
 
+LATE_MIX = 1
+LATE_OUT = 2
+PIECES = 2
+
 
 def dot(a, b, ca=1, cb=0):
     return lax.dot_general(a, b, (((ca,), (cb,)), ((), ())), preferred_element_type=F32)
 
 
-def dot_rows(a, b, cut):
-    return jnp.concatenate([dot(a[:cut], b), dot(a[cut:], b)], axis=0)
-
-
-def halo_mix(recv_ref, spread_ref, c, top):
+def halo_mix(recv_ref, spread_ref, mix_ref, total_ref, c, top):
     halo = jnp.concatenate([recv_ref[0, c], recv_ref[1, c]], axis=1)
-    return dot(halo[:top], spread_ref[0]), dot(halo, spread_ref[1])
+    total_ref[c, :top] = (mix_ref[c, :top] + dot(halo[:top], spread_ref[0])).astype(BF16)
+    total_ref[c, top:] = (mix_ref[c, top:] + dot(halo, spread_ref[1])).astype(BF16)
 
 
 def step_kernel(
@@ -56,8 +57,7 @@
     gain_ref,
     syn_turned,
     coef_ref,
-    tail_ref,
-    head_ref,
+    edge_ref,
     pick_all,
     coup_all,
     gain_all,
@@ -93,9 +93,9 @@
         peer = lax.rem(sec + hop, n_sec)
         pl.semaphore_signal(barrier, inc=1, device_id=(ves, peer), device_id_type=MESH)
 
-    def halo_copy(src, side, part, to):
+    def halo_copy(side, part, to):
         return pltpu.make_async_remote_copy(
-            src_ref=src.at[part],
+            src_ref=edge_ref.at[side, part],
             dst_ref=recv_ref.at[side, part],
             send_sem=send_sem.at[side],
             recv_sem=recv_sem.at[side, part],
@@ -104,15 +104,15 @@
         )
 
     def up_copy(c):
-        return halo_copy(tail_ref, 0, c, ves + 1)
+        return halo_copy(0, c, ves + 1)
 
     def down_copy(c):
-        return halo_copy(head_ref, 1, c, ves - 1)
+        return halo_copy(1, c, ves - 1)
 
     turn = lax.rem(ves, 4)
     up_first = (turn == 0)
     greet_stage = jnp.where(ves == 0, jnp.where(sec == 0, 4, 2), jnp.where(turn == 0, 2, jnp.where(turn == 1, 0, jnp.where(turn == 2, 0, 0))))
-    second_stage = jnp.where(ves == 0, jnp.where(sec == 0, 4, 3), jnp.where(turn == 0, 5, jnp.where(turn == 1, jnp.where(sec == 0, 2, 4), jnp.where(turn == 2, 3, 3))))
+    second_stage = jnp.where(ves == 0, 4, jnp.where(turn == 0, jnp.where(sec == 0, 3, 4), jnp.where(turn == 1, jnp.where(sec == 0, 3, 4), jnp.where(turn == 2, 3, 3))))
 
     def send(c, lead, when):
         up = up_first if lead else jnp.logical_not(up_first)
@@ -136,7 +136,7 @@
                 send(c, True, greet_stage <= stage)
             elif c < stage:
                 send(c, True, greet_stage == stage)
-        if stage >= comps - 1:
+        if stage >= comps:
             for c in range(comps):
                 send(c, False, second_stage == stage)
 
@@ -195,20 +195,40 @@
 
         low = lax.broadcasted_iota(jnp.int32, (cut, tile), 1) < edge
         load_ana.wait()
-        ana = ana_ref[...]
-
-        for c in range(comps):
+
+        def analyse(c, lanes):
+            dens = dens_ref[c, :, lanes]
+            return jnp.concatenate([dot(ana_ref[:top], dens), dot(ana_ref[top:], dens)], axis=0)
+
+        def pack(part, upward):
+            turned = pltpu.roll(part, edge, 1)
+            tail = jnp.where(low, turned[:cut], part[top:])
+            head = jnp.where(low, part[:cut], turned[top:])
+            if upward is True or upward is False:
+                return (tail if upward else head).astype(BF16)
+            return jnp.where(upward, tail, head).astype(BF16)
+
+        def analyse_side(upward):
+            lanes = pl.ds(pl.multiple_of(jnp.where(upward, tile, 0), tile), tile)
+            part = analyse(0, lanes)
+            edge_ref[jnp.where(upward, 0, 1), 0] = pack(part, upward)
+            return lanes, part
+
+        load_dens[0].wait()
+        lanes, part = analyse_side(up_first)
+        at_stage(0)
+        coef_ref[0, :, lanes] = part.astype(BF16)
+        load_syn.start()
+        load_near.start()
+        for c in range(1, comps):
             load_dens[c].wait()
-            full = dot_rows(ana, dens_ref[c], top)
+            full = analyse(c, slice(None))
             coef_ref[c] = full.astype(BF16)
-            head = full[:, :tile]
-            tail = full[:, count - tile :]
-            tail_ref[c] = jnp.where(low, pltpu.roll(tail, edge, 1)[:cut], tail[top:]).astype(BF16)
-            head_ref[c] = jnp.where(low, head[:cut], pltpu.roll(head, edge, 1)[top:]).astype(BF16)
-            if c == 0:
-                load_syn.start()
-                load_near.start()
+            edge_ref[0, c] = pack(full[:, count - tile :], True)
+            edge_ref[1, c] = pack(full[:, :tile], False)
             at_stage(c)
+        lanes, part = analyse_side(jnp.logical_not(up_first))
+        coef_ref[0, :, lanes] = part.astype(BF16)
 
         base = (ves * n_sec + sec) * count
 
@@ -262,9 +282,8 @@
 
         load_syn.wait()
         syn_turned[...] = syn_ref[...].T
-        syn = syn_turned[...]
         load_near.wait()
-        both_ref[...] = dot(near_ref[...].T, syn).astype(BF16)
+        both_ref[...] = dot(near_ref[...].T, syn_turned[...]).astype(BF16)
         at_stage(comps + 2)
 
         for hop in hops:
@@ -281,7 +300,9 @@
             back = dot(coup, dens, 1, 1).astype(BF16)
             wall = dot(back, place, 0, 0)
             scaled = coef_ref[c].astype(F32) * gain
-            out_ref[c] = dot_rows(syn, (scaled + wall).astype(BF16), half)
+            own = (scaled + wall).astype(BF16)
+            out_ref[c, :half] = dot(syn_turned[:half], own)
+            out_ref[c, half:] = dot(syn_turned[half:], own)
 
     pl.run_scoped(
         work,
@@ -299,62 +320,63 @@
         def _():
             down_copy(c).wait_recv()
 
-        if c < comps - 1:
-            first, second = halo_mix(recv_ref, spread_ref, c, top)
-            total_ref[:top] = (mix_ref[c, :top] + first).astype(BF16)
-            total_ref[top:] = (mix_ref[c, top:] + second).astype(BF16)
-        if c < comps - 2:
-            out_ref[c] = out_ref[c] + dot_rows(both_ref[...], total_ref[...], half)
+        if c < comps - LATE_MIX:
+            halo_mix(recv_ref, spread_ref, mix_ref, total_ref, c, top)
+        if c < comps - LATE_OUT:
+            out_ref[c, :half] = out_ref[c, :half] + dot(both_ref[:half], total_ref[c])
+            out_ref[c, half:] = out_ref[c, half:] + dot(both_ref[half:], total_ref[c])
+
+    def sent(side, to):
+        return pltpu.make_async_remote_copy(
+            src_ref=edge_ref.at[side],
+            dst_ref=recv_ref.at[side],
+            send_sem=send_sem.at[side],
+            recv_sem=recv_sem.at[side, 0],
+            device_id=(to, sec),
+            device_id_type=MESH,
+        )
 
     @pl.when(has_right)
     def _():
-        pltpu.make_async_remote_copy(
-            src_ref=tail_ref, dst_ref=recv_ref.at[0], send_sem=send_sem.at[0], recv_sem=recv_sem.at[0, 0],
-            device_id=(ves + 1, sec), device_id_type=MESH,
-        ).wait_send()
+        sent(0, ves + 1).wait_send()
 
     @pl.when(has_left)
     def _():
-        pltpu.make_async_remote_copy(
-            src_ref=head_ref, dst_ref=recv_ref.at[1], send_sem=send_sem.at[1], recv_sem=recv_sem.at[1, 0],
-            device_id=(ves - 1, sec), device_id_type=MESH,
-        ).wait_send()
+        sent(1, ves - 1).wait_send()
 
 
 def finish_kernel(
     part_ref,
     both_ref,
     mix_ref,
-    total_ref,
+    early_ref,
     spread_ref,
     recv_ref,
     out_ref,
     result_ref,
-    last_ref,
+    total_ref,
     done_sem,
     piece_sem,
 ):
     comps, num_points, _ = part_ref.shape
-    last = comps - 1
+    early = comps - LATE_OUT
+    mixed = comps - LATE_MIX
     top = mix_ref.shape[1] - recv_ref.shape[2]
-    half = num_points // 2
+    rows = num_points // PIECES
     stores = [
-        pltpu.make_async_copy(part_ref.at[c], out_ref.at[c], done_sem.at[c])
-        for c in range(comps - 2)
+        pltpu.make_async_copy(part_ref.at[c], out_ref.at[c], done_sem.at[c]) for c in range(early)
     ]
     for store in stores:
         store.start()
-    first, second = halo_mix(recv_ref, spread_ref, last, top)
-    last_ref[:top] = (mix_ref[last, :top] + first).astype(BF16)
-    last_ref[top:] = (mix_ref[last, top:] + second).astype(BF16)
-    for k, source in enumerate((total_ref, last_ref)):
-        c = comps - 2 + k
-        total = source[...]
-        for i in range(2):
-            rows = pl.ds(i * half, half)
-            result_ref[k, rows] = part_ref[c, rows] + dot(both_ref[rows], total)
+    for c in range(mixed, comps):
+        halo_mix(recv_ref, spread_ref, mix_ref, total_ref, c, top)
+    for c in range(early, comps):
+        total = (early_ref if c < mixed else total_ref)[c]
+        for i in range(PIECES):
+            part = pl.ds(i * rows, rows)
+            result_ref[c - early, part] = part_ref[c, part] + dot(both_ref[part], total)
             store = pltpu.make_async_copy(
-                result_ref.at[k, rows], out_ref.at[c, rows], piece_sem.at[k, i]
+                result_ref.at[c - early, part], out_ref.at[c, part], piece_sem.at[c - early, i]
             )
             store.start()
             stores.append(store)
@@ -392,7 +414,7 @@
             jax.ShapeDtypeStruct((comps, num_points, count), F32),
             jax.ShapeDtypeStruct((num_points, num_coefs), BF16),
             jax.ShapeDtypeStruct((comps, num_coefs, count), F32),
-            jax.ShapeDtypeStruct((num_coefs, count), BF16),
+            jax.ShapeDtypeStruct((comps, num_coefs, count), BF16),
             jax.ShapeDtypeStruct((2, 2 * tile, count), BF16),
             jax.ShapeDtypeStruct((2, comps, cut, tile), BF16),
         ),
@@ -411,8 +433,7 @@
             pltpu.VMEM((num_coefs,), F32),
             pltpu.VMEM((num_points, num_coefs), BF16),
             pltpu.VMEM((comps, num_coefs, count), BF16),
-            pltpu.VMEM((comps, cut, tile), BF16),
-            pltpu.VMEM((comps, cut, tile), BF16),
+            pltpu.VMEM((2, comps, cut, tile), BF16),
             pltpu.VMEM((n_sec, comps, near_wall, num_coefs), BF16),
             pltpu.VMEM((others, region_wall, panels), BF16),
             pltpu.VMEM((others, 1, panels), F32),
@@ -447,10 +468,10 @@
         in_specs=[vmem] * 6,
         out_specs=pl.BlockSpec(memory_space=pltpu.HBM),
         scratch_shapes=[
-            pltpu.VMEM((2, num_points, count), F32),
-            pltpu.VMEM((num_coefs, count), BF16),
-            pltpu.SemaphoreType.DMA((comps - 2,)),
-            pltpu.SemaphoreType.DMA((2, 2)),
+            pltpu.VMEM((LATE_OUT, num_points, count), F32),
+            pltpu.VMEM((comps, num_coefs, count), BF16),
+            pltpu.SemaphoreType.DMA((comps - LATE_OUT,)),
+            pltpu.SemaphoreType.DMA((LATE_OUT, PIECES)),
         ],
         compiler_params=pltpu.CompilerParams(vmem_limit_bytes=16 * 1024 * 1024),
     )(*middle)

time: 10.3 us -> 10.2 us (level)
  no operation moved by 1% of the time
where the time goes in v3:
time: 10.2 us; the launch traced here: 10 us
  Pallas kernels  10 us (98%)
    pallas_call x1, Pallas kernels, shards(): pl.pallas_call(functools.partial(step_kernel, n_ves, n_sec), name='vesicl...  8.64 us
    pallas_call x1, Pallas kernels, shards(): pl.pallas_call(finish_kernel, name='vesicle_finish', out_shape=jax.ShapeD...  1.39 us

profile of v3, /device:TPU:4, one launch (start us, length us, event | category | flops | bytes accessed | tf_op | source)
XLA Modules:
  0.0 10.0 jit_solution(2704160364123066504)
XLA Ops:
  0.0 8.6 %vesicle_step.1 = (f32[3,544,256]{2,1,0:T(8,128)S(1)}, bf16[544,289]{1,0:T(8,128)(2,1)S(1)}, f32[3,289,256]{2,1,0:T(8,128)S(1)}, bf16[3,289,256]{2,1,0:T(8,128)(...) custom-call(bf16[3,544,256]{2,1,0:T(8,128)(2,1)} %bitcast.7, bf16[289,544]{1,0:T(8,128)(2,1)} %bitcast.8, ...), custom_call_target="tpu_custom_call" | custom-call | tf_op jit(solution)/shard_map/vesicle_step/pallas_call | solution.py:410
  8.6 1.4 %vesicle_finish.1 = f32[3,544,256]{2,1,0:T(8,128)} custom-call(f32[3,544,256]{2,1,0:T(8,128)S(1)} %get-tuple-element.11.part_ref, bf16[544,289]{1,0:T(8,128)(2,1)S(1)} %get-tuple-element.12.both_ref, f32[3,289,256]{2,1,0:T(8,128)S(1)} %get-tuple-element.13.mix_ref, bf16[3,289,256]{2,1,0:T(8,128)(2,1)S(1)} %get-tuple-element.14.early_ref, ...), custom_call_target="tpu_custom_call" | custom-call | tf_op jit(solution)/shard_map/vesicle_finish/pallas_call | solution.py:464

commit v4 on v3

--- a/solution.py
+++ b/solution.py
@@ -13,7 +13,7 @@
 
 LATE_MIX = 1
 LATE_OUT = 2
-PIECES = 2
+PIECES = 4
 
 
 def dot(a, b, ca=1, cb=0):
@@ -81,24 +81,25 @@
 
     barrier = pltpu.get_barrier_semaphore()
 
-    @pl.when(has_left)
-    def _():
-        pl.semaphore_signal(barrier, inc=1, device_id=(ves - 1, sec), device_id_type=MESH)
-
-    @pl.when(has_right)
-    def _():
-        pl.semaphore_signal(barrier, inc=1, device_id=(ves + 1, sec), device_id_type=MESH)
-
-    for hop in hops:
-        peer = lax.rem(sec + hop, n_sec)
-        pl.semaphore_signal(barrier, inc=1, device_id=(ves, peer), device_id_type=MESH)
+    def announce():
+        @pl.when(has_left)
+        def _():
+            pl.semaphore_signal(barrier, inc=1, device_id=(ves - 1, sec), device_id_type=MESH)
+
+        @pl.when(has_right)
+        def _():
+            pl.semaphore_signal(barrier, inc=1, device_id=(ves + 1, sec), device_id_type=MESH)
+
+        for hop in hops:
+            peer = lax.rem(sec + hop, n_sec)
+            pl.semaphore_signal(barrier, inc=1, device_id=(ves, peer), device_id_type=MESH)
 
     def halo_copy(side, part, to):
         return pltpu.make_async_remote_copy(
             src_ref=edge_ref.at[side, part],
             dst_ref=recv_ref.at[side, part],
-            send_sem=send_sem.at[side],
-            recv_sem=recv_sem.at[side, part],
+            send_sem=send_sem.at[0],
+            recv_sem=recv_sem.at[part],
             device_id=(to, sec),
             device_id_type=MESH,
         )
@@ -156,7 +157,10 @@
         loads = [
             pltpu.make_async_copy(src, dst, load_sem.at[i]) for i, (src, dst) in enumerate(pairs)
         ]
-        for load in loads[:-2]:
+        for load in loads[:2]:
+            load.start()
+        announce()
+        for load in loads[2:-2]:
             load.start()
         load_ana, *load_dens = loads[: comps + 1]
         load_list, load_part, load_weight, load_coup, load_wgain, load_gain, load_syn, load_near = (
@@ -310,15 +314,27 @@
         pltpu.SemaphoreType.DMA((3, max(n_sec - 1, 1))),
     )
 
+    inner = has_left & has_right
+
+    def pair(parts, c):
+        return pltpu.make_async_remote_copy(
+            src_ref=edge_ref.at[:, parts],
+            dst_ref=recv_ref.at[:, parts],
+            send_sem=send_sem.at[0],
+            recv_sem=recv_sem.at[c],
+            device_id=(ves, sec),
+            device_id_type=MESH,
+        )
+
     for c in range(comps):
 
-        @pl.when(has_left)
+        @pl.when(inner)
+        def _():
+            pair(pl.ds(c, 1), c).wait_recv()
+
+        @pl.when(jnp.logical_not(inner))
         def _():
             up_copy(c).wait_recv()
-
-        @pl.when(has_right)
-        def _():
-            down_copy(c).wait_recv()
 
         if c < comps - LATE_MIX:
             halo_mix(recv_ref, spread_ref, mix_ref, total_ref, c, top)
@@ -326,23 +342,20 @@
             out_ref[c, :half] = out_ref[c, :half] + dot(both_ref[:half], total_ref[c])
             out_ref[c, half:] = out_ref[c, half:] + dot(both_ref[half:], total_ref[c])
 
-    def sent(side, to):
-        return pltpu.make_async_remote_copy(
-            src_ref=edge_ref.at[side],
-            dst_ref=recv_ref.at[side],
-            send_sem=send_sem.at[side],
-            recv_sem=recv_sem.at[side, 0],
-            device_id=(to, sec),
+    @pl.when(inner)
+    def _():
+        pair(pl.ds(0, comps), 0).wait_send()
+
+    @pl.when(jnp.logical_not(inner))
+    def _():
+        pltpu.make_async_remote_copy(
+            src_ref=edge_ref.at[0],
+            dst_ref=recv_ref.at[0],
+            send_sem=send_sem.at[0],
+            recv_sem=recv_sem.at[0],
+            device_id=(ves, sec),
             device_id_type=MESH,
-        )
-
-    @pl.when(has_right)
-    def _():
-        sent(0, ves + 1).wait_send()
-
-    @pl.when(has_left)
-    def _():
-        sent(1, ves - 1).wait_send()
+        ).wait_send()
 
 
 def finish_kernel(
@@ -437,8 +450,8 @@
             pltpu.VMEM((n_sec, comps, near_wall, num_coefs), BF16),
             pltpu.VMEM((others, region_wall, panels), BF16),
             pltpu.VMEM((others, 1, panels), F32),
-            pltpu.SemaphoreType.DMA((2,)),
-            pltpu.SemaphoreType.DMA((2, comps)),
+            pltpu.SemaphoreType.DMA((1,)),
+            pltpu.SemaphoreType.DMA((comps,)),
             pltpu.SemaphoreType.DMA((3, others)),
         ],
         compiler_params=pltpu.CompilerParams(

time: 10.2 us -> 10.2 us (level)
  no operation moved by 1% of the time
where the time goes in v4:
time: 10.2 us; the launch traced here: 9.96 us
  Pallas kernels  9.95 us (98%)
    pallas_call x1, Pallas kernels, shards(): pl.pallas_call(functools.partial(step_kernel, n_ves, n_sec), name='vesicl...  8.6 us
    pallas_call x1, Pallas kernels, shards(): pl.pallas_call(finish_kernel, name='vesicle_finish', out_shape=jax.ShapeD...  1.35 us

profile of v4, /device:TPU:4, one launch (start us, length us, event | category | flops | bytes accessed | tf_op | source)
XLA Modules:
  0.0 10.0 jit_solution(11477648749073186139)
XLA Ops:
  0.0 8.6 %vesicle_step.1 = (f32[3,544,256]{2,1,0:T(8,128)S(1)}, bf16[544,289]{1,0:T(8,128)(2,1)S(1)}, f32[3,289,256]{2,1,0:T(8,128)S(1)}, bf16[3,289,256]{2,1,0:T(8,128)(...) custom-call(bf16[3,544,256]{2,1,0:T(8,128)(2,1)} %bitcast.7, bf16[289,544]{1,0:T(8,128)(2,1)} %bitcast.8, ...), custom_call_target="tpu_custom_call" | custom-call | tf_op jit(solution)/shard_map/vesicle_step/pallas_call | solution.py:423
  8.6 1.3 %vesicle_finish.1 = f32[3,544,256]{2,1,0:T(8,128)} custom-call(f32[3,544,256]{2,1,0:T(8,128)S(1)} %get-tuple-element.11.part_ref, bf16[544,289]{1,0:T(8,128)(2,1)S(1)} %get-tuple-element.12.both_ref, f32[3,289,256]{2,1,0:T(8,128)S(1)} %get-tuple-element.13.mix_ref, bf16[3,289,256]{2,1,0:T(8,128)(2,1)S(1)} %get-tuple-element.14.early_ref, ...), custom_call_target="tpu_custom_call" | custom-call | tf_op jit(solution)/shard_map/vesicle_finish/pallas_call | solution.py:477

commit v5 on v4

--- a/solution.py
+++ b/solution.py
@@ -367,7 +367,6 @@
     recv_ref,
     out_ref,
     result_ref,
-    total_ref,
     done_sem,
     piece_sem,
 ):
@@ -381,10 +380,14 @@
     ]
     for store in stores:
         store.start()
+    late = []
     for c in range(mixed, comps):
-        halo_mix(recv_ref, spread_ref, mix_ref, total_ref, c, top)
+        halo = jnp.concatenate([recv_ref[0, c], recv_ref[1, c]], axis=1)
+        upper = (mix_ref[c, :top] + dot(halo[:top], spread_ref[0])).astype(BF16)
+        lower = (mix_ref[c, top:] + dot(halo, spread_ref[1])).astype(BF16)
+        late.append(jnp.concatenate([upper, lower], axis=0))
     for c in range(early, comps):
-        total = (early_ref if c < mixed else total_ref)[c]
+        total = early_ref[c] if c < mixed else late[c - mixed]
         for i in range(PIECES):
             part = pl.ds(i * rows, rows)
             result_ref[c - early, part] = part_ref[c, part] + dot(both_ref[part], total)
@@ -482,7 +485,6 @@
         out_specs=pl.BlockSpec(memory_space=pltpu.HBM),
         scratch_shapes=[
             pltpu.VMEM((LATE_OUT, num_points, count), F32),
-            pltpu.VMEM((comps, num_coefs, count), BF16),
             pltpu.SemaphoreType.DMA((comps - LATE_OUT,)),
             pltpu.SemaphoreType.DMA((LATE_OUT, PIECES)),
         ],

time: 10.2 us -> 10.2 us (level)
  no operation moved by 1% of the time
where the time goes in v5:
time: 10.2 us; the launch traced here: 9.96 us
  Pallas kernels  9.95 us (98%)
    pallas_call x1, Pallas kernels, shards(): pl.pallas_call(functools.partial(step_kernel, n_ves, n_sec), name='vesicl...  8.6 us
    pallas_call x1, Pallas kernels, shards(): pl.pallas_call(finish_kernel, name='vesicle_finish', out_shape=jax.ShapeD...  1.35 us

profile of v5, /device:TPU:4, one launch (start us, length us, event | category | flops | bytes accessed | tf_op | source)
XLA Modules:
  0.0 10.0 jit_solution(773674310353429326)
XLA Ops:
  0.0 8.6 %vesicle_step.1 = (f32[3,544,256]{2,1,0:T(8,128)S(1)}, bf16[544,289]{1,0:T(8,128)(2,1)S(1)}, f32[3,289,256]{2,1,0:T(8,128)S(1)}, bf16[3,289,256]{2,1,0:T(8,128)(...) custom-call(bf16[3,544,256]{2,1,0:T(8,128)(2,1)} %bitcast.7, bf16[289,544]{1,0:T(8,128)(2,1)} %bitcast.8, ...), custom_call_target="tpu_custom_call" | custom-call | tf_op jit(solution)/shard_map/vesicle_step/pallas_call | solution.py:426
  8.6 1.3 %vesicle_finish.1 = f32[3,544,256]{2,1,0:T(8,128)} custom-call(f32[3,544,256]{2,1,0:T(8,128)S(1)} %get-tuple-element.11.part_ref, bf16[544,289]{1,0:T(8,128)(2,1)S(1)} %get-tuple-element.12.both_ref, f32[3,289,256]{2,1,0:T(8,128)S(1)} %get-tuple-element.13.mix_ref, bf16[3,289,256]{2,1,0:T(8,128)(2,1)S(1)} %get-tuple-element.14.early_ref, ...), custom_call_target="tpu_custom_call" | custom-call | tf_op jit(solution)/shard_map/vesicle_finish/pallas_call | solution.py:480

commit v6 on v5

--- a/solution.py
+++ b/solution.py
@@ -139,7 +139,8 @@
                 send(c, True, greet_stage == stage)
         if stage >= comps:
             for c in range(comps):
-                send(c, False, second_stage == stage)
+                spread = (turn == 3) & (sec == 1) if c == comps - 1 else False
+                send(c, False, jnp.where(spread, 4, second_stage) == stage)
 
     def work(load_sem, wall_send):
         pairs = [(ana_in, ana_ref)]

time: 10.2 us -> 10.2 us (level)
  no operation moved by 1% of the time
where the time goes in v6:
time: 10.2 us; the launch traced here: 9.96 us
  Pallas kernels  9.95 us (98%)
    pallas_call x1, Pallas kernels, shards(): pl.pallas_call(functools.partial(step_kernel, n_ves, n_sec), name='vesicl...  8.6 us
    pallas_call x1, Pallas kernels, shards(): pl.pallas_call(finish_kernel, name='vesicle_finish', out_shape=jax.ShapeD...  1.35 us

profile of v6, /device:TPU:4, one launch (start us, length us, event | category | flops | bytes accessed | tf_op | source)
XLA Modules:
  0.0 10.0 jit_solution(12117550374969261534)
XLA Ops:
  0.0 8.6 %vesicle_step.1 = (f32[3,544,256]{2,1,0:T(8,128)S(1)}, bf16[544,289]{1,0:T(8,128)(2,1)S(1)}, f32[3,289,256]{2,1,0:T(8,128)S(1)}, bf16[3,289,256]{2,1,0:T(8,128)(...) custom-call(bf16[3,544,256]{2,1,0:T(8,128)(2,1)} %bitcast.7, bf16[289,544]{1,0:T(8,128)(2,1)} %bitcast.8, ...), custom_call_target="tpu_custom_call" | custom-call | tf_op jit(solution)/shard_map/vesicle_step/pallas_call | solution.py:427
  8.6 1.3 %vesicle_finish.1 = f32[3,544,256]{2,1,0:T(8,128)} custom-call(f32[3,544,256]{2,1,0:T(8,128)S(1)} %get-tuple-element.11.part_ref, bf16[544,289]{1,0:T(8,128)(2,1)S(1)} %get-tuple-element.12.both_ref, f32[3,289,256]{2,1,0:T(8,128)S(1)} %get-tuple-element.13.mix_ref, bf16[3,289,256]{2,1,0:T(8,128)(2,1)S(1)} %get-tuple-element.14.early_ref, ...), custom_call_target="tpu_custom_call" | custom-call | tf_op jit(solution)/shard_map/vesicle_finish/pallas_call | solution.py:481
